TPU v7x, 32 devices: a whole 2x2x4 slice. The times are simulated.
32 devices in a mesh: seq: 8 (over z, y), head: 4 (over x, core).
Axes of the slice: x: 2, y: 2, z: 4, core: 2. Of those that a mesh axis runs over, the one named last changes fastest.
Arguments:
- queries: bfloat16 [8192, 4096], P('seq', 'head'), may hold values from -6 to 6
- keys: bfloat16 [8192, 4096], P('seq', 'head'), may hold values from -6 to 6
- values: bfloat16 [8192, 4096], P('seq', 'head'), may hold values from -6 to 6
- out_grad: bfloat16 [8192, 4096], P('seq', 'head'), may hold values from -6 to 6
- level_table: float32 [4, 256], replicated, may hold values from 0.05 to 0.5
- table_index: int32 [8192], P('seq'), may hold values from 0 to 255
- reach: int32 [8], P('seq'), may hold values from 1 to 3, as said below
Outputs:
- query_grad: bfloat16 [8192, 4096], P('seq', 'head')
- key_grad: bfloat16 [8192, 4096], P('seq', 'head')
- value_grad: bfloat16 [8192, 4096], P('seq', 'head')
- table_grad: float32 [4, 256], replicated
Inputs may be any that keep to these rules, and one draw needn't show every extreme that they name: Some group has reach 3 and some has reach 1.
All inputs are finite; a program needn't handle non-finite values.
Results may differ from a plain program's by a relative error of at most 0.0056.
Values sent between devices are 32-bit elements; how exact they have to be, the bound alone decides.
A program may use at most 128 MiB of HBM per device.

v0:
```python
import functools

import jax
import jax.numpy as jnp
from jax import lax
from jax.experimental import pallas as pl
from jax.experimental.pallas import tpu as pltpu
from jax.sharding import PartitionSpec as P

DH = 128
BLOCK = 256
CHUNKS = 4

HOP = 2.2
GAP = 1.4
LAG = 0.0
MESH = pl.DeviceIdType.MESH
f32 = jnp.float32
bf16 = jnp.bfloat16
NN = (((1,), (0,)), ((), ()))
NT = (((1,), (1,)), ((), ()))
TN = (((0,), (0,)), ((), ()))


def mul(a, b, dims):
    return lax.dot_general(a, b, dims, preferred_element_type=f32)


def split(x):
    high = x.astype(bf16)
    rest = x - high.astype(f32)
    middle = rest.astype(bf16)
    return [high, middle, (rest - middle.astype(f32)).astype(bf16)]


def kernel(
    span, wide, count, levels, heads, length,
    q_hbm, k_hbm, v_hbm, g_hbm, table_ref, index_ref, reach_ref,
    dq_out, dk_out, dv_out, tab_out,
    qb, kb, vb, gb, dqn, dkn, dvn,
    fs, fr, bs, br, acc, stbf, rbf,
    wrow, wcol, lam_near, lam_far, tab1, tab2,
    in_sem, fsend, frecv, bsend, brecv, t1send, t1recv, t2send, t2recv,
):
    me = lax.axis_index("seq")
    mine = lax.axis_index("head")
    scale = 1.0 / DH
    per = heads // CHUNKS
    ntab = table_ref.shape[1]
    blocks = length // BLOCK

    def load(which, src, dst, h):
        return pltpu.make_async_copy(src.at[:, pl.ds(h * DH, DH)], dst.at[h], in_sem.at[which, h])

    ins = ((2, g_hbm, gb), (3, q_hbm, qb), (0, v_hbm, vb), (1, k_hbm, kb))
    for h in range(heads):
        for which, src, dst in ins:
            load(which, src, dst, h).start()

    barrier = pltpu.get_barrier_semaphore()
    for off in range(1, span):
        pl.semaphore_signal(barrier, inc=1, device_id={"seq": (me + off) % span}, device_id_type=MESH)
    for off in range(1, wide):
        pl.semaphore_signal(barrier, inc=1, device_id={"head": (mine + off) % wide}, device_id_type=MESH)

    top, low = levels - 1, levels - 2
    step = 2 ** low
    quarter = me // step
    bits = [(me // 2 ** b) % 2 for b in range(levels)]
    odd = bits[low] == 1
    even = bits[low] == 0
    f_sends, f_gets, b_sends, b_gets, f_to, b_to = [], [], [], [], [], []
    for b in range(levels):
        partner = me + (1 - 2 * bits[b]) * 2 ** b
        if b < low:
            clear_above = (me // 2 ** (b + 1)) < (span // 2 ** (b + 1) - 1)
            sends = jnp.logical_or(bits[b] == 0, clear_above)
            gets = jnp.logical_or(bits[b] == 1, clear_above)
            f_sends.append(sends)
            f_gets.append(gets)
            b_sends.append(gets)
            b_gets.append(sends)
            f_to.append(partner)
            b_to.append(partner)
        else:
            inner = jnp.logical_or(quarter == 1, quarter == 2)
            f_sends.append(even if b == low else inner)
            f_gets.append(odd if b == low else quarter >= 2)
            b_sends.append(odd if b == low else quarter >= 2)
            b_gets.append(even if b == low else inner)
            f_to.append((me + step) % span)
            b_to.append((me + span - step) % span)

    def part(c):
        return pl.ds(c * per, per)

    def f_copy(b, c, relay=False):
        src = fr if relay else fs
        return pltpu.make_async_remote_copy(
            src_ref=src.at[b, part(c)], dst_ref=fr.at[b, part(c)], send_sem=fsend.at[b, c], recv_sem=frecv.at[b, c],
            device_id={"seq": f_to[b]}, device_id_type=MESH)

    def b_copy(b, c):
        return pltpu.make_async_remote_copy(
            src_ref=bs.at[b, part(c)], dst_ref=br.at[b, part(c)], send_sem=bsend.at[b, c], recv_sem=brecv.at[b, c],
            device_id={"seq": b_to[b]}, device_id_type=MESH)

    def f_start(b, c):
        @pl.when(f_sends[b])
        def _():
            f_copy(b, c).start()

    def b_start(b, c):
        @pl.when(b_sends[b])
        def _():
            b_copy(b, c).start()

    def f_keep(b, c):
        stbf[part(c), :, pl.ds(b * DH, DH)] = fr[b, part(c)].astype(bf16)

    def f_stage(b, c):
        @pl.when(f_gets[b])
        def _():
            f_copy(b, c).wait_recv()
            fs[b + 1, part(c)] = fs[b, part(c)] + fr[b, part(c)]

        f_start(b + 1, c)

        @pl.when(bits[b] == 1)
        def _():
            f_keep(b, c)

    def f_hop(c):
        @pl.when(odd)
        def _():
            f_copy(low, c).wait_recv()
            f_keep(low, c)

        @pl.when(quarter == 1)
        def _():
            fs[top, part(c)] = fs[low, part(c)] + fr[low, part(c)]
            f_copy(top, c).start()

    def f_relay(c):
        @pl.when(quarter == 2)
        def _():
            f_copy(top, c).wait_recv()
            f_copy(top, c, True).start()
            f_keep(top, c)

    def f_last(c):
        @pl.when(quarter == 3)
        def _():
            f_copy(top, c).wait_recv()
            f_keep(top, c)

    def b_next(b, c):
        bs[b, part(c)] = bs[b, part(c)] + acc[part(c)]
        b_start(b, c)

    def b_relay(c):
        @pl.when(quarter == 2)
        def _():
            b_copy(top, c).wait_recv()
            bs[top, part(c)] = bs[top, part(c)] + br[top, part(c)]
            b_copy(top, c).start()

    def b_turn(c):
        @pl.when(quarter == 1)
        def _():
            b_copy(top, c).wait_recv()
            acc[part(c)] = br[top, part(c)]
            bs[low, part(c)] = bs[low, part(c)] + br[top, part(c)]
            b_copy(low, c).start()
            b_next(low - 1, c)

    def b_hop(c):
        @pl.when(even)
        def _():
            b_copy(low, c).wait_recv()
            acc[part(c)] = br[low, part(c)]
            b_next(low - 1, c)

    def b_stage(b, c):
        @pl.when(b_gets[b])
        def _():
            b_copy(b, c).wait_recv()
            acc[part(c)] = acc[part(c)] + br[b, part(c)]

        if b > 0:
            b_next(b - 1, c)
        else:
            rbf[part(c)] = acc[part(c)].astype(bf16)

    def state_step(h, carry):
        load(0, v_hbm, vb, h).wait()
        load(1, k_hbm, kb, h).wait()
        fs[0, h] = mul(vb[h], kb[h], TN)
        return carry

    def part_step(h, carry):
        load(2, g_hbm, gb, h).wait()
        load(3, q_hbm, qb, h).wait()
        q = qb[h].astype(f32)
        weighted = jnp.concatenate([(q * wcol[l]).astype(bf16) for l in range(levels)], 1)
        whole = mul(gb[h], weighted, TN)
        for l in range(levels):
            bs[l, h] = whole[:, l * DH:(l + 1) * DH] * bits[l].astype(f32)
        return carry

    acc[...] = jnp.zeros(acc.shape, f32)
    stbf[...] = jnp.zeros(stbf.shape, bf16)
    lam_near[...] = jnp.zeros(lam_near.shape, f32)
    lam_far[...] = jnp.zeros(lam_far.shape, f32)
    onehot = (lax.broadcasted_iota(jnp.int32, (ntab, length), 0) == index_ref[...]).astype(f32).astype(bf16)
    rows = sum(mul(x, onehot, NN) for x in split(table_ref[...]))
    active = (lax.broadcasted_iota(jnp.int32, (levels + 1, 1), 0) <= reach_ref[0]).astype(f32)
    rows = rows * active
    wrow[...] = rows[0:1] * scale
    lane_level = lax.broadcasted_iota(jnp.int32, (levels + 1, levels * DH), 1) // DH + 1
    pick = (lax.broadcasted_iota(jnp.int32, (levels + 1, levels * DH), 0) == lane_level).astype(f32).astype(bf16)
    spread = mul(jnp.concatenate(split(rows), 0), jnp.concatenate([pick] * 3, 0), TN)
    for l in range(levels):
        wcol[l] = spread[:, l * DH:(l + 1) * DH]

    for c in range(CHUNKS):
        lax.fori_loop(c * per, (c + 1) * per, part_step, 0)
        lax.fori_loop(c * per, (c + 1) * per, state_step, 0)
        if c == 0:
            pl.semaphore_wait(barrier, span - 1 + wide - 1)
        f_start(0, c)

        @pl.when(quarter == 3)
        def _():
            b_copy(top, c).start()
            b_start(low - 1, c)
    for c in range(CHUNKS):
        @pl.when(quarter == 3)
        def _():
            b_copy(low, c).start()

    timed = []
    for c in range(CHUNKS):
        for b in range(low):
            timed.append((HOP * (b + 1) + GAP * c, functools.partial(f_stage, b), c))
        base = HOP * low + GAP * c
        timed.append((base + HOP, f_hop, c))
        timed.append((base + 2 * HOP, f_relay, c))
        timed.append((base + 3 * HOP, f_last, c))
        base = LAG + GAP * c
        timed.append((base + HOP, b_relay, c))
        timed.append((base + 2 * HOP, b_turn, c))
        timed.append((base + 3 * HOP, b_hop, c))
    timed.sort(key=lambda item: item[0])
    inside = [(max(0, int(when)), run, c) for when, run, c in timed if when < heads]
    after = [(run, c) for when, run, c in timed if when >= heads]

    def near_step(h, carry):
        for slot in sorted({item[0] for item in inside}):
            @pl.when(h == slot)
            def _():
                for when, run, c in inside:
                    if when == slot:
                        run(c)

        causal = lax.broadcasted_iota(jnp.int32, (BLOCK, BLOCK), 1) >= lax.broadcasted_iota(jnp.int32, (BLOCK, BLOCK), 0)
        for j in range(blocks):
            start, stop = j * BLOCK, (j + 1) * BLOCK
            rest = length - start
            k_j = kb[h, start:stop]
            v_j = vb[h, start:stop]
            q_r = qb[h, start:]
            g_r = gb[h, start:]
            scores = mul(k_j, q_r, NT)
            grads = mul(v_j, g_r, NT)
            s_parts, g_parts = [], []
            for i in range(rest // BLOCK):
                s_i = scores[:, i * BLOCK:(i + 1) * BLOCK]
                g_i = grads[:, i * BLOCK:(i + 1) * BLOCK]
                if i == 0:
                    s_i = jnp.where(causal, s_i, 0.0)
                    g_i = jnp.where(causal, g_i, 0.0)
                at = slice(start + i * BLOCK, start + (i + 1) * BLOCK)
                w_i = wrow[:, at]
                lam_near[:, at] += jnp.sum((s_i * g_i).reshape(BLOCK // 8, 8, BLOCK), axis=0)
                s_parts.append((s_i * w_i).astype(bf16))
                g_parts.append((g_i * w_i).astype(bf16))
            probs = jnp.concatenate(s_parts, 1)
            gsc = jnp.concatenate(g_parts, 1)
            dvn[h, start:stop] = mul(probs, g_r, NN)
            dkn[h, start:stop] = mul(gsc, q_r, NN)
            dq = mul(gsc, k_j, TN)
            if j == 0:
                dqn[h] = dq
            else:
                dqn[h, start:] += dq
        return carry

    lax.fori_loop(0, heads, near_step, 0)

    def query_step(h, carry):
        cols = pl.ds(pl.multiple_of(h * DH, DH), DH)
        for i in range(blocks):
            at = slice(i * BLOCK, (i + 1) * BLOCK)
            reads = mul(gb[h, at], stbf[h], NN)
            q = qb[h, at].astype(f32)
            far = None
            for l in range(levels):
                read = reads[:, l * DH:(l + 1) * DH]
                lam_far[l, at] += q * read
                term = read * wcol[l, at]
                far = term if far is None else far + term
            dq_out[at, cols] = (dqn[h, at] + scale * far).astype(bf16)
        return carry

    def key_step(h, carry):
        cols = pl.ds(pl.multiple_of(h * DH, DH), DH)
        for i in range(blocks):
            at = slice(i * BLOCK, (i + 1) * BLOCK)
            dk_out[at, cols] = (dkn[h, at] + scale * mul(vb[h, at], rbf[h], NN)).astype(bf16)
            dv_out[at, cols] = (dvn[h, at] + scale * mul(kb[h, at], rbf[h], NT)).astype(bf16)
        return carry

    for c in range(CHUNKS):
        while any(run is f_last and late <= c for run, late in after):
            run, late = after.pop(0)
            run(late)
        lax.fori_loop(c * per, (c + 1) * per, query_step, 0)
    for run, late in after:
        run(late)

    onehot = (lax.broadcasted_iota(jnp.int32, (ntab, length), 0) == index_ref[...]).astype(f32).astype(bf16)
    near_row = jnp.sum(lam_near[...], axis=0, keepdims=True)
    near_sum = sum(mul(x, onehot, NT) for x in split(near_row))
    lane = lax.broadcasted_iota(jnp.int32, (length, DH), 1)
    columns = jnp.zeros((length, DH), f32)
    for l in range(levels):
        columns = jnp.where(lane == l, jnp.sum(lam_far[l], axis=1, keepdims=True), columns)
    far_sum = sum(mul(onehot, x, NN) for x in split(columns)).T
    tab1[me] = jnp.concatenate([near_sum, far_sum[0:levels]], 0) * active * (scale / count)

    def t1_copy(off):
        return pltpu.make_async_remote_copy(
            src_ref=tab1.at[me], dst_ref=tab1.at[me], send_sem=t1send.at[off], recv_sem=t1recv.at[off],
            device_id={"seq": (me + off) % span}, device_id_type=MESH)

    def t1_from(off):
        place = (me + span - off) % span
        return pltpu.make_async_remote_copy(
            src_ref=tab1.at[place], dst_ref=tab1.at[place], send_sem=t1send.at[off], recv_sem=t1recv.at[off],
            device_id={"seq": (me + off) % span}, device_id_type=MESH)

    def t2_copy(off):
        return pltpu.make_async_remote_copy(
            src_ref=tab2.at[mine], dst_ref=tab2.at[mine], send_sem=t2send.at[off], recv_sem=t2recv.at[off],
            device_id={"head": (mine + off) % wide}, device_id_type=MESH)

    def t2_from(off):
        place = (mine + wide - off) % wide
        return pltpu.make_async_remote_copy(
            src_ref=tab2.at[place], dst_ref=tab2.at[place], send_sem=t2send.at[off], recv_sem=t2recv.at[off],
            device_id={"head": (mine + off) % wide}, device_id_type=MESH)

    for c in range(CHUNKS):
        for b in range(low - 1, -1, -1):
            b_stage(b, c)
        if c == 0:
            for off in range(1, span):
                t1_copy(off).start()
        lax.fori_loop(c * per, (c + 1) * per, key_step, 0)
        if c == CHUNKS - 2:
            for off in range(1, span):
                t1_from(off).wait_recv()
            total = tab1[0]
            for s in range(1, span):
                total = total + tab1[s]
            tab2[mine] = total
        if c == CHUNKS - 1:
            for off in range(1, wide):
                t2_from(off).wait_recv()
            total = tab2[0]
            for s in range(1, wide):
                total = total + tab2[s]
            tab_out[...] = total
        elif c == CHUNKS - 2:
            for off in range(1, wide):
                t2_copy(off).start()

    for off in range(1, span):
        t1_copy(off).wait_send()
    for off in range(1, wide):
        t2_copy(off).wait_send()
    for b in range(levels):
        for c in range(CHUNKS):
            @pl.when(f_sends[b])
            def _():
                f_copy(b, c).wait_send()

            @pl.when(b_sends[b])
            def _():
                b_copy(b, c).wait_send()


def local(queries, keys, values, out_grad, level_table, table_index, reach):
    length = queries.shape[0]
    heads = queries.shape[1] // DH
    levels = level_table.shape[0] - 1
    span = lax.axis_size("seq")
    wide = lax.axis_size("head")
    any_spec = pl.BlockSpec(memory_space=pl.ANY)
    vmem = pl.BlockSpec(memory_space=pltpu.VMEM)
    dma = pltpu.SemaphoreType.DMA
    big = jax.ShapeDtypeStruct(queries.shape, bf16)
    body = functools.partial(kernel, span, wide, length * span, levels, heads, length)
    strip = (heads, length, DH)
    square = (levels, heads, DH, DH)
    return pl.pallas_call(
        body,
        out_shape=(big, big, big, jax.ShapeDtypeStruct(level_table.shape, f32)),
        in_specs=[any_spec] * 4 + [vmem, vmem, pl.BlockSpec(memory_space=pltpu.SMEM)],
        out_specs=(vmem, vmem, vmem, vmem),
        scratch_shapes=[
            pltpu.VMEM(strip, bf16), pltpu.VMEM(strip, bf16), pltpu.VMEM(strip, bf16), pltpu.VMEM(strip, bf16),
            pltpu.VMEM(strip, f32), pltpu.VMEM(strip, f32), pltpu.VMEM(strip, f32),
            pltpu.VMEM(square, f32), pltpu.VMEM(square, f32), pltpu.VMEM(square, f32), pltpu.VMEM(square, f32),
            pltpu.VMEM((heads, DH, DH), f32),
            pltpu.VMEM((heads, DH, levels * DH), bf16),
            pltpu.VMEM((heads, DH, DH), bf16),
            pltpu.VMEM((1, length), f32),
            pltpu.VMEM((levels, length, DH), f32),
            pltpu.VMEM((8, length), f32),
            pltpu.VMEM((levels, length, DH), f32),
            pltpu.VMEM((span,) + level_table.shape, f32),
            pltpu.VMEM((wide,) + level_table.shape, f32),
            dma((4, heads)),
            dma((levels, CHUNKS)), dma((levels, CHUNKS)), dma((levels, CHUNKS)), dma((levels, CHUNKS)),
            dma((span,)), dma((span,)), dma((wide,)), dma((wide,)),
        ],
        compiler_params=pltpu.CompilerParams(
            collective_id=0, has_side_effects=True, vmem_limit_bytes=46 * 2 ** 20
        ),
        name="loglinear",
    )(queries, keys, values, out_grad, level_table, table_index.reshape(1, length), reach)


def solution(mesh):
    return jax.shard_map(
        local,
        mesh=mesh,
        in_specs=(
            P("seq", "head"),
            P("seq", "head"),
            P("seq", "head"),
            P("seq", "head"),
            P(),
            P("seq"),
            P("seq"),
        ),
        out_specs=(P("seq", "head"), P("seq", "head"), P("seq", "head"), P()),
        check_vma=False,
    )
```

profile of v0, /device:TPU:0, one launch (start us, length us, event | category | flops | bytes accessed | tf_op | source)
XLA Modules:
  0.0 55.4 jit_solution(8184155348595284791)
XLA Ops:
  1.3 0.0 copy-start
  1.3 0.7 %copy-done = f32[4,256]{1,0:T(4,128)S(1)} copy-done((f32[4,256]{1,0:T(4,128)S(1)}, f32[4,256]{1,0:T(4,128)}, u32[]{:S(2)}) %copy-start) | copy-done | bytes 4120
  2.0 0.0 copy-start.1
  2.0 0.7 %copy-done.1 = s32[1024]{0:T(1024)S(1)} copy-done((s32[1024]{0:T(1024)S(1)}, s32[1024]{0:T(1024)}, u32[]{:S(2)}) %copy-start.1) | copy-done | bytes 4120
  2.7 48.1 %loglinear.1 = (bf16[1024,1024]{1,0:T(8,128)(2,1)S(1)}, bf16[1024,1024]{1,0:T(8,128)(2,1)S(1)}, bf16[1024,1024]{1,0:T(8,128)(2,1)S(1)}, f32[4,256]{1,0:T(4,128)S(1)}) custom-call(bf16[1024,1024]{1,0:T(8,128)(2,1)} %q_hbm.1, bf16[1024,1024]{1,0:T(8,128)(2,1)} %k_hbm.1, bf16[1024,1024]{1,0:T(8,128)(2,1)} %v_hbm.1, bf16[1024,1024]{1,0:T(8,128)(2,1)} %g_hbm.1, ...), custom_call_target="tpu_custom_call" | custom-call | tf_op jit(solution)/shard_map/loglinear/pallas_call | solution.py:417
  50.8 1.3 %copy.16 = bf16[1024,1024]{1,0:T(8,128)(2,1)} copy(bf16[1024,1024]{1,0:T(8,128)(2,1)S(1)} %get-tuple-element.8) | data formatting | bytes 4194304
  52.1 1.3 %copy.17 = bf16[1024,1024]{1,0:T(8,128)(2,1)} copy(bf16[1024,1024]{1,0:T(8,128)(2,1)S(1)} %get-tuple-element.9) | data formatting | bytes 4194304
  53.4 1.3 %copy.18 = bf16[1024,1024]{1,0:T(8,128)(2,1)} copy(bf16[1024,1024]{1,0:T(8,128)(2,1)S(1)} %get-tuple-element.10) | data formatting | bytes 4194304
  54.8 0.6 %copy.19 = f32[4,256]{1,0:T(4,128)} copy(f32[4,256]{1,0:T(4,128)S(1)} %get-tuple-element.11) | data formatting | bytes 8192
Async XLA Ops:
  1.3 0.7 %copy-start = (f32[4,256]{1,0:T(4,128)S(1)}, f32[4,256]{1,0:T(4,128)}, u32[]{:S(2)}) copy-start(f32[4,256]{1,0:T(4,128)} %table_ref.1) | copy-start | bytes 12292
  2.0 0.7 %copy-start.1 = (s32[1024]{0:T(1024)S(1)}, s32[1024]{0:T(1024)}, u32[]{:S(2)}) copy-start(s32[1024]{0:T(1024)} %param.12) | copy-start | bytes 12292
where the time goes:
time: 55.6 us; the launch traced here: 55.4 us
  Pallas kernels  48.1 us (87%)
  local copies, waits for them, and re-layouts  5.92 us (11%)
  between operations  1.3 us (2%)
    pallas_call x1, Pallas kernels, local(): pl.pallas_call(body, out_shape=(big, big, big, jax.ShapeDtypeStruct(level...  48.1 us
    unnamed x8, local copies, waits for them, and re-layouts  5.92 us

commit v1 on v0

--- a/solution.py
+++ b/solution.py
@@ -10,6 +10,7 @@
 DH = 128
 BLOCK = 256
 CHUNKS = 4
+PIECES = 1
 
 HOP = 2.2
 GAP = 1.4
@@ -39,7 +40,7 @@
     dq_out, dk_out, dv_out, tab_out,
     qb, kb, vb, gb, dqn, dkn, dvn,
     fs, fr, bs, br, acc, stbf, rbf,
-    wrow, wcol, lam_near, lam_far, tab1, tab2,
+    wrow, wcol, lam_near, lam_far, tab1, tab2, onehot,
     in_sem, fsend, frecv, bsend, brecv, t1send, t1recv, t2send, t2recv,
 ):
     me = lax.axis_index("seq")
@@ -212,8 +213,8 @@
     stbf[...] = jnp.zeros(stbf.shape, bf16)
     lam_near[...] = jnp.zeros(lam_near.shape, f32)
     lam_far[...] = jnp.zeros(lam_far.shape, f32)
-    onehot = (lax.broadcasted_iota(jnp.int32, (ntab, length), 0) == index_ref[...]).astype(f32).astype(bf16)
-    rows = sum(mul(x, onehot, NN) for x in split(table_ref[...]))
+    onehot[...] = (lax.broadcasted_iota(jnp.int32, (ntab, length), 0) == index_ref[...]).astype(f32).astype(bf16)
+    rows = sum(mul(x, onehot[...], NN) for x in split(table_ref[...]))
     active = (lax.broadcasted_iota(jnp.int32, (levels + 1, 1), 0) <= reach_ref[0]).astype(f32)
     rows = rows * active
     wrow[...] = rows[0:1] * scale
@@ -297,6 +298,9 @@
         return carry
 
     lax.fori_loop(0, heads, near_step, 0)
+    near_row = jnp.sum(lam_near[...], axis=0, keepdims=True)
+    near_sum = mul(jnp.concatenate(split(near_row), 0), onehot[...], NT)
+    tab1[me, 0:1] = jnp.sum(near_sum, axis=0, keepdims=True)
 
     def query_step(h, carry):
         cols = pl.ds(pl.multiple_of(h * DH, DH), DH)
@@ -329,15 +333,15 @@
     for run, late in after:
         run(late)
 
-    onehot = (lax.broadcasted_iota(jnp.int32, (ntab, length), 0) == index_ref[...]).astype(f32).astype(bf16)
-    near_row = jnp.sum(lam_near[...], axis=0, keepdims=True)
-    near_sum = sum(mul(x, onehot, NT) for x in split(near_row))
     lane = lax.broadcasted_iota(jnp.int32, (length, DH), 1)
     columns = jnp.zeros((length, DH), f32)
     for l in range(levels):
-        columns = jnp.where(lane == l, jnp.sum(lam_far[l], axis=1, keepdims=True), columns)
-    far_sum = sum(mul(onehot, x, NN) for x in split(columns)).T
-    tab1[me] = jnp.concatenate([near_sum, far_sum[0:levels]], 0) * active * (scale / count)
+        columns = jnp.where(lane % levels == l, jnp.sum(lam_far[l], axis=1, keepdims=True), columns)
+    thirds = split(columns)
+    third = jnp.where(lane < levels, thirds[0].astype(f32), jnp.where(lane < 2 * levels, thirds[1].astype(f32), thirds[2].astype(f32)))
+    turned = mul(onehot[...], third.astype(bf16), NN).T
+    far_sum = turned[0:levels] + turned[levels:2 * levels] + turned[2 * levels:3 * levels]
+    tab1[me] = jnp.concatenate([tab1[me, 0:1], far_sum], 0) * active * (scale / count)
 
     def t1_copy(off):
         return pltpu.make_async_remote_copy(
@@ -401,6 +405,22 @@
                 b_copy(b, c).wait_send()
 
 
+def finish(*refs):
+    sem = refs[-1]
+    half = (len(refs) - 1) // 2
+    copies = []
+    for src, dst in zip(refs[:half], refs[half:-1]):
+        pieces = PIECES if src.shape[0] > DH else 1
+        rows = src.shape[0] // pieces
+        for piece in range(pieces):
+            at = pl.ds(piece * rows, rows)
+            copies.append(pltpu.make_async_copy(src.at[at], dst.at[at], sem.at[len(copies)]))
+    for copy in copies:
+        copy.start()
+    for copy in copies:
+        copy.wait()
+
+
 def local(queries, keys, values, out_grad, level_table, table_index, reach):
     length = queries.shape[0]
     heads = queries.shape[1] // DH
@@ -411,12 +431,14 @@
     vmem = pl.BlockSpec(memory_space=pltpu.VMEM)
     dma = pltpu.SemaphoreType.DMA
     big = jax.ShapeDtypeStruct(queries.shape, bf16)
+    outs = (big, big, big, jax.ShapeDtypeStruct(level_table.shape, f32))
+    hbm = pl.BlockSpec(memory_space=pltpu.HBM)
     body = functools.partial(kernel, span, wide, length * span, levels, heads, length)
     strip = (heads, length, DH)
     square = (levels, heads, DH, DH)
-    return pl.pallas_call(
+    parts = pl.pallas_call(
         body,
-        out_shape=(big, big, big, jax.ShapeDtypeStruct(level_table.shape, f32)),
+        out_shape=outs,
         in_specs=[any_spec] * 4 + [vmem, vmem, pl.BlockSpec(memory_space=pltpu.SMEM)],
         out_specs=(vmem, vmem, vmem, vmem),
         scratch_shapes=[
@@ -432,6 +454,7 @@
             pltpu.VMEM((levels, length, DH), f32),
             pltpu.VMEM((span,) + level_table.shape, f32),
             pltpu.VMEM((wide,) + level_table.shape, f32),
+            pltpu.VMEM((level_table.shape[1], length), bf16),
             dma((4, heads)),
             dma((levels, CHUNKS)), dma((levels, CHUNKS)), dma((levels, CHUNKS)), dma((levels, CHUNKS)),
             dma((span,)), dma((span,)), dma((wide,)), dma((wide,)),
@@ -441,6 +464,15 @@
         ),
         name="loglinear",
     )(queries, keys, values, out_grad, level_table, table_index.reshape(1, length), reach)
+    return pl.pallas_call(
+        finish,
+        out_shape=outs,
+        in_specs=[vmem] * 4,
+        out_specs=(hbm, hbm, hbm, hbm),
+        scratch_shapes=[dma((3 * PIECES + 1,))],
+        compiler_params=pltpu.CompilerParams(vmem_limit_bytes=2 ** 20),
+        name="finish",
+    )(*parts)
 
 
 def solution(mesh):

time: 55.6 us -> 53.3 us (0.959)
  local copies, waits for them, and re-layouts: 5.92 us -> 1.37 us
  Pallas kernels: 48.1 us -> 50.4 us
    unnamed x8 -> x4, local copies, waits for them, and re-layouts: 5.92 us -> 1.37 us
    pallas_call x1 -> x2, Pallas kernels: 48.1 us -> 50.4 us  [the longest x1 47.7 us: local(): pl.pallas_call(body, out_shape=outs, in_specs=[any_spec] * 4 + [vmem, vme...]
where the time goes in v1:
time: 53.3 us; the launch traced here: 53.1 us
  Pallas kernels  50.4 us (95%)
  local copies, waits for them, and re-layouts  1.37 us (3%)
  between operations  1.3 us (2%)
    pallas_call x1, Pallas kernels, local(): pl.pallas_call(body, out_shape=outs, in_specs=[any_spec] * 4 + [vmem, vme...  47.7 us
    pallas_call x1, Pallas kernels, local(): pl.pallas_call(finish, out_shape=outs, in_specs=[vmem] * 4, out_specs=(hb...  2.74 us
    unnamed x4, local copies, waits for them, and re-layouts  1.37 us

profile of v1, /device:TPU:0, one launch (start us, length us, event | category | flops | bytes accessed | tf_op | source)
XLA Modules:
  0.0 53.1 jit_solution(7518581111149177630)
XLA Ops:
  1.3 0.0 copy-start
  1.3 0.7 %copy-done = f32[4,256]{1,0:T(4,128)S(1)} copy-done((f32[4,256]{1,0:T(4,128)S(1)}, f32[4,256]{1,0:T(4,128)}, u32[]{:S(2)}) %copy-start) | copy-done | bytes 4120
  2.0 0.0 copy-start.1
  2.0 0.7 %copy-done.1 = s32[1024]{0:T(1024)S(1)} copy-done((s32[1024]{0:T(1024)S(1)}, s32[1024]{0:T(1024)}, u32[]{:S(2)}) %copy-start.1) | copy-done | bytes 4120
  2.7 47.7 %loglinear.1 = (bf16[1024,1024]{1,0:T(8,128)(2,1)S(1)}, bf16[1024,1024]{1,0:T(8,128)(2,1)S(1)}, bf16[1024,1024]{1,0:T(8,128)(2,1)S(1)}, f32[4,256]{1,0:T(4,128)S(1)}) custom-call(bf16[1024,1024]{1,0:T(8,128)(2,1)} %q_hbm.1, bf16[1024,1024]{1,0:T(8,128)(2,1)} %k_hbm.1, bf16[1024,1024]{1,0:T(8,128)(2,1)} %v_hbm.1, bf16[1024,1024]{1,0:T(8,128)(2,1)} %g_hbm.1, ...), custom_call_target="tpu_custom_call" | custom-call | tf_op jit(solution)/shard_map/loglinear/pallas_call | solution.py:439
  50.4 2.7 %finish.1 = (bf16[1024,1024]{1,0:T(8,128)(2,1)}, bf16[1024,1024]{1,0:T(8,128)(2,1)}, bf16[1024,1024]{1,0:T(8,128)(2,1)}, f32[4,256]{1,0:T(4,128)}) custom-call(bf16[1024,1024]{1,0:T(8,128)(2,1)S(1)} %get-tuple-element.8.refs_0_, bf16[1024,1024]{1,0:T(8,128)(2,1)S(1)} %get-tuple-element.9.refs_1_, bf16[1024,1024]{1,0:T(8,128)(2,1)S(1)} %get-tuple-element.10.refs_2_, ...), custom_call_target="tpu_custom_call" | custom-call | tf_op jit(solution)/shard_map/finish/pallas_call | solution.py:467
Async XLA Ops:
  1.3 0.7 %copy-start = (f32[4,256]{1,0:T(4,128)S(1)}, f32[4,256]{1,0:T(4,128)}, u32[]{:S(2)}) copy-start(f32[4,256]{1,0:T(4,128)} %table_ref.1) | copy-start | bytes 12292
  2.0 0.7 %copy-start.1 = (s32[1024]{0:T(1024)S(1)}, s32[1024]{0:T(1024)}, u32[]{:S(2)}) copy-start(s32[1024]{0:T(1024)} %param.12) | copy-start | bytes 12292

commit v2 on v1

--- a/solution.py
+++ b/solution.py
@@ -15,6 +15,7 @@
 HOP = 2.2
 GAP = 1.4
 LAG = 0.0
+LEAD = 1.0
 MESH = pl.DeviceIdType.MESH
 f32 = jnp.float32
 bf16 = jnp.bfloat16
@@ -41,7 +42,7 @@
     qb, kb, vb, gb, dqn, dkn, dvn,
     fs, fr, bs, br, acc, stbf, rbf,
     wrow, wcol, lam_near, lam_far, tab1, tab2, onehot,
-    in_sem, fsend, frecv, bsend, brecv, t1send, t1recv, t2send, t2recv,
+    in_sem, know, fsend, frecv, bsend, brecv, t1send, t1recv, t2send, t2recv,
 ):
     me = lax.axis_index("seq")
     mine = lax.axis_index("head")
@@ -58,18 +59,39 @@
         for which, src, dst in ins:
             load(which, src, dst, h).start()
 
-    barrier = pltpu.get_barrier_semaphore()
-    for off in range(1, span):
-        pl.semaphore_signal(barrier, inc=1, device_id={"seq": (me + off) % span}, device_id_type=MESH)
-    for off in range(1, wide):
-        pl.semaphore_signal(barrier, inc=1, device_id={"head": (mine + off) % wide}, device_id_type=MESH)
-
     top, low = levels - 1, levels - 2
     step = 2 ** low
     quarter = me // step
     bits = [(me // 2 ** b) % 2 for b in range(levels)]
     odd = bits[low] == 1
     even = bits[low] == 0
+    inner = jnp.logical_or(quarter == 1, quarter == 2)
+    up, down = (me + step) % span, (me + span - step) % span
+    partners = [me + (1 - 2 * bits[b]) * 2 ** b for b in range(low)]
+
+    def greet(sem):
+        for partner in partners:
+            pl.semaphore_signal(sem, inc=1, device_id={"seq": partner}, device_id_type=MESH)
+
+        @pl.when(quarter < 3)
+        def _():
+            pl.semaphore_signal(sem, inc=1, device_id={"seq": up}, device_id_type=MESH)
+
+        @pl.when(quarter > 0)
+        def _():
+            pl.semaphore_signal(sem, inc=1, device_id={"seq": down}, device_id_type=MESH)
+
+    near_by = low + 1 + inner.astype(jnp.int32)
+    barrier = pltpu.get_barrier_semaphore()
+    greet(barrier)
+    for off in range(1, wide):
+        pl.semaphore_signal(barrier, inc=1, device_id={"head": (mine + off) % wide}, device_id_type=MESH)
+
+    def hear(r):
+        pl.semaphore_wait(know.at[r], near_by)
+        if r + 1 < low + 2:
+            greet(know.at[r + 1])
+
     f_sends, f_gets, b_sends, b_gets, f_to, b_to = [], [], [], [], [], []
     for b in range(levels):
         partner = me + (1 - 2 * bits[b]) * 2 ** b
@@ -228,7 +250,8 @@
         lax.fori_loop(c * per, (c + 1) * per, part_step, 0)
         lax.fori_loop(c * per, (c + 1) * per, state_step, 0)
         if c == 0:
-            pl.semaphore_wait(barrier, span - 1 + wide - 1)
+            pl.semaphore_wait(barrier, near_by + wide - 1)
+            greet(know.at[0])
         f_start(0, c)
 
         @pl.when(quarter == 3)
@@ -243,15 +266,17 @@
     timed = []
     for c in range(CHUNKS):
         for b in range(low):
-            timed.append((HOP * (b + 1) + GAP * c, functools.partial(f_stage, b), c))
-        base = HOP * low + GAP * c
-        timed.append((base + HOP, f_hop, c))
-        timed.append((base + 2 * HOP, f_relay, c))
+            timed.append((HOP * (b + 1) + GAP * c - LEAD, functools.partial(f_stage, b), c))
+        base = HOP * low + GAP * c - LEAD
+        timed.append((min(base + HOP, heads + 0.4 + 0.01 * c), f_hop, c))
+        timed.append((min(base + 2 * HOP, heads + 0.5 + 0.01 * c), f_relay, c))
         timed.append((base + 3 * HOP, f_last, c))
         base = LAG + GAP * c
         timed.append((base + HOP, b_relay, c))
         timed.append((base + 2 * HOP, b_turn, c))
         timed.append((base + 3 * HOP, b_hop, c))
+    for r in range(low + 2):
+        timed.append((2.0 + r, lambda c, r=r: hear(r), 0))
     timed.sort(key=lambda item: item[0])
     inside = [(max(0, int(when)), run, c) for when, run, c in timed if when < heads]
     after = [(run, c) for when, run, c in timed if when >= heads]
@@ -331,7 +356,8 @@
             run(late)
         lax.fori_loop(c * per, (c + 1) * per, query_step, 0)
     for run, late in after:
-        run(late)
+        if run is not b_hop:
+            run(late)
 
     lane = lax.broadcasted_iota(jnp.int32, (length, DH), 1)
     columns = jnp.zeros((length, DH), f32)
@@ -365,12 +391,14 @@
             src_ref=tab2.at[place], dst_ref=tab2.at[place], send_sem=t2send.at[off], recv_sem=t2recv.at[off],
             device_id={"head": (mine + off) % wide}, device_id_type=MESH)
 
+    for off in range(1, span):
+        t1_copy(off).start()
+    for run, late in after:
+        if run is b_hop:
+            run(late)
     for c in range(CHUNKS):
         for b in range(low - 1, -1, -1):
             b_stage(b, c)
-        if c == 0:
-            for off in range(1, span):
-                t1_copy(off).start()
         lax.fori_loop(c * per, (c + 1) * per, key_step, 0)
         if c == CHUNKS - 2:
             for off in range(1, span):
@@ -456,6 +484,7 @@
             pltpu.VMEM((wide,) + level_table.shape, f32),
             pltpu.VMEM((level_table.shape[1], length), bf16),
             dma((4, heads)),
+            pltpu.SemaphoreType.REGULAR((levels,)),
             dma((levels, CHUNKS)), dma((levels, CHUNKS)), dma((levels, CHUNKS)), dma((levels, CHUNKS)),
             dma((span,)), dma((span,)), dma((wide,)), dma((wide,)),
         ],

time: 53.3 us -> 51.4 us (0.964)
  Pallas kernels: 50.4 us -> 48.5 us
    pallas_call x1, Pallas kernels: 47.7 us -> 45.7 us  [local(): pl.pallas_call(body, out_shape=outs, in_specs=[any_spec] * 4 + [vmem, vme...]
where the time goes in v2:
time: 51.4 us; the launch traced here: 51.1 us
  Pallas kernels  48.5 us (94%)
  local copies, waits for them, and re-layouts  1.37 us (3%)
  between operations  1.3 us (3%)
    pallas_call x1, Pallas kernels, local(): pl.pallas_call(body, out_shape=outs, in_specs=[any_spec] * 4 + [vmem, vme...  45.7 us
    pallas_call x1, Pallas kernels, local(): pl.pallas_call(finish, out_shape=outs, in_specs=[vmem] * 4, out_specs=(hb...  2.74 us
    unnamed x4, local copies, waits for them, and re-layouts  1.37 us

profile of v2, /device:TPU:0, one launch (start us, length us, event | category | flops | bytes accessed | tf_op | source)
XLA Modules:
  0.0 51.1 jit_solution(1862487347285033710)
XLA Ops:
  1.3 0.0 copy-start
  1.3 0.7 %copy-done = f32[4,256]{1,0:T(4,128)S(1)} copy-done((f32[4,256]{1,0:T(4,128)S(1)}, f32[4,256]{1,0:T(4,128)}, u32[]{:S(2)}) %copy-start) | copy-done | bytes 4120
  2.0 0.0 copy-start.1
  2.0 0.7 %copy-done.1 = s32[1024]{0:T(1024)S(1)} copy-done((s32[1024]{0:T(1024)S(1)}, s32[1024]{0:T(1024)}, u32[]{:S(2)}) %copy-start.1) | copy-done | bytes 4120
  2.7 45.7 %loglinear.1 = (bf16[1024,1024]{1,0:T(8,128)(2,1)S(1)}, bf16[1024,1024]{1,0:T(8,128)(2,1)S(1)}, bf16[1024,1024]{1,0:T(8,128)(2,1)S(1)}, f32[4,256]{1,0:T(4,128)S(1)}) custom-call(bf16[1024,1024]{1,0:T(8,128)(2,1)} %q_hbm.1, bf16[1024,1024]{1,0:T(8,128)(2,1)} %k_hbm.1, bf16[1024,1024]{1,0:T(8,128)(2,1)} %v_hbm.1, bf16[1024,1024]{1,0:T(8,128)(2,1)} %g_hbm.1, ...), custom_call_target="tpu_custom_call" | custom-call | tf_op jit(solution)/shard_map/loglinear/pallas_call | solution.py:467
  48.4 2.7 %finish.1 = (bf16[1024,1024]{1,0:T(8,128)(2,1)}, bf16[1024,1024]{1,0:T(8,128)(2,1)}, bf16[1024,1024]{1,0:T(8,128)(2,1)}, f32[4,256]{1,0:T(4,128)}) custom-call(bf16[1024,1024]{1,0:T(8,128)(2,1)S(1)} %get-tuple-element.8.refs_0_, bf16[1024,1024]{1,0:T(8,128)(2,1)S(1)} %get-tuple-element.9.refs_1_, bf16[1024,1024]{1,0:T(8,128)(2,1)S(1)} %get-tuple-element.10.refs_2_, ...), custom_call_target="tpu_custom_call" | custom-call | tf_op jit(solution)/shard_map/finish/pallas_call | solution.py:496
Async XLA Ops:
  1.3 0.7 %copy-start = (f32[4,256]{1,0:T(4,128)S(1)}, f32[4,256]{1,0:T(4,128)}, u32[]{:S(2)}) copy-start(f32[4,256]{1,0:T(4,128)} %table_ref.1) | copy-start | bytes 12292
  2.0 0.7 %copy-start.1 = (s32[1024]{0:T(1024)S(1)}, s32[1024]{0:T(1024)}, u32[]{:S(2)}) copy-start(s32[1024]{0:T(1024)} %param.12) | copy-start | bytes 12292
